TPU v7x, 128 devices: a whole 4x4x4 slice. The times are simulated.
128 devices in a mesh: section: 8 (over x, core), expert: 16 (over z, y).
Axes of the slice: x: 4, y: 4, z: 4, core: 2. Of those that a mesh axis runs over, the one named last changes fastest.
Arguments:
- sent_acts: bfloat16 [8, 2048, 6144], P('section', 'expert'), may hold values from -6 to 6
- sent_cots: bfloat16 [8, 2048, 6144], P('section', 'expert'), may hold values from -6 to 6
- expert_ids: int32 [8, 2048, 2], P('section', 'expert'), may hold values from 0 to 7, as said below
- gate_probs: float32 [8, 2048, 2], P('section', 'expert'), may hold values from 0.1 to 0.9
- gate_weight: bfloat16 [8, 6144, 8192], P('section', None, 'expert'), may hold values from -0.078125 to 0.078125
- up_weight: bfloat16 [8, 6144, 8192], P('section', None, 'expert'), may hold values from -0.078125 to 0.078125
- down_weight: bfloat16 [8, 8192, 6144], P('section', 'expert'), may hold values from -0.0625 to 0.0625
Outputs:
- out_acts: bfloat16 [8, 2048, 6144], P('section', 'expert')
- in_grads: bfloat16 [8, 2048, 6144], P('section', 'expert')
Inputs may be any that keep to these rules, and one draw needn't show every extreme that they name: `expert_ids`: in every section, at most 40 of the 128 tokens of one device name expert 0, and at least one device's tokens name it 40 times; a token's two experts differ.
All inputs are finite; a program needn't handle non-finite values.
Results may differ from a plain program's by a relative error of at most 0.015.
Values may be sent and summed in bfloat16 or wider, within the bound.
A program may use at most 128 MiB of HBM per device.

v0:
```python
import jax
import jax.numpy as jnp
from jax import lax
from jax.sharding import PartitionSpec as P

CAP = 40


def shifted(value, axis, steps):
    count = lax.axis_size(axis)
    pairs = [(source, (source + steps) % count) for source in range(count)]
    return lax.ppermute(value, axis, pairs)


def silu_grad(pre):
    sigma = jax.nn.sigmoid(pre)
    return sigma * (1.0 + pre * (1.0 - sigma))


def run_rows(kernel, inputs):
    return kernel(*inputs)


def combine(term_rows):
    return lax.psum_scatter(
        term_rows(jnp.int32(0), lax.axis_size("expert") * CAP).astype(jnp.bfloat16),
        "expert",
        scatter_dimension=0,
        tiled=True,
    ).astype(jnp.float32)


def body(sent_acts, sent_cots, expert_ids, gate_probs, gate_weight, up_weight, down_weight):
    tok_count = sent_acts.shape[1]
    gate_cols = gate_weight[0]
    up_cols = up_weight[0]
    down_rows = down_weight[0]
    contract = (((1,), (1,)), ((), ()))
    incoming = shifted(sent_acts[0], "section", 1)
    cot_in = shifted(sent_cots[0], "section", -1)
    chosen = expert_ids[0] == 0
    picked = jnp.any(chosen, axis=1)
    picked_int = picked.astype(jnp.int32)
    share = jnp.sum(jnp.where(chosen, gate_probs[0], 0.0), axis=1)
    ranking = jnp.cumsum(picked_int) - picked_int
    slot_of = jnp.where(picked, ranking, CAP)
    table = (
        jnp.full((CAP + 1,), -1, jnp.int32)
        .at[slot_of]
        .set(jnp.arange(tok_count, dtype=jnp.int32))[:CAP]
    )
    filled_slot = table >= 0
    source = jnp.maximum(table, 0)
    slot_acts = jnp.where(filled_slot[:, None], incoming[source], jnp.zeros((), incoming.dtype))
    all_acts = lax.all_gather(slot_acts, "expert", axis=0, tiled=True)

    def forward_rows(rows_in):
        pre_gate = jnp.dot(rows_in, gate_cols, preferred_element_type=jnp.float32)
        pre_up = jnp.dot(rows_in, up_cols, preferred_element_type=jnp.float32)
        hidden = (jax.nn.silu(pre_gate) * pre_up).astype(jnp.bfloat16)
        return (pre_gate, pre_up, hidden)

    pre_gate, pre_up, hidden = run_rows(forward_rows, (all_acts,))

    def forward_term(start, count):
        return jnp.dot(hidden, down_rows, preferred_element_type=jnp.float32)

    slot_out = combine(forward_term)
    back_index = jnp.minimum(slot_of, CAP - 1)
    out_acts = jnp.where(picked[:, None], share[:, None] * slot_out[back_index], 0.0).astype(
        jnp.bfloat16
    )
    out_grad = (cot_in.astype(jnp.float32) * share[:, None]).astype(jnp.bfloat16)
    slot_grads = jnp.where(filled_slot[:, None], out_grad[source], jnp.zeros((), out_grad.dtype))
    all_grads = lax.all_gather(slot_grads, "expert", axis=0, tiled=True)

    def backward_rows(gate_in, up_in, grads_in):
        hid_grad = lax.dot_general(
            grads_in, down_rows, contract, preferred_element_type=jnp.float32
        )
        gate_grad = (hid_grad * up_in * silu_grad(gate_in)).astype(jnp.bfloat16)
        up_grad = (hid_grad * jax.nn.silu(gate_in)).astype(jnp.bfloat16)
        return (gate_grad, up_grad)

    gate_grad, up_grad = run_rows(backward_rows, (pre_gate, pre_up, all_grads))

    def backward_term(start, count):
        term = lax.dot_general(gate_grad, gate_cols, contract, preferred_element_type=jnp.float32)
        return term + lax.dot_general(
            up_grad, up_cols, contract, preferred_element_type=jnp.float32
        )

    slot_back = combine(backward_term)
    in_grads = jnp.where(picked[:, None], slot_back[back_index], 0.0).astype(jnp.bfloat16)
    return (out_acts[None], in_grads[None])


def solution(mesh):
    placed = (
        P("section", "expert", None),
        P("section", "expert", None),
        P("section", "expert", None),
        P("section", "expert", None),
        P("section", None, "expert"),
        P("section", None, "expert"),
        P("section", "expert", None),
    )
    return jax.shard_map(
        body,
        mesh=mesh,
        in_specs=placed,
        out_specs=(P("section", "expert", None), P("section", "expert", None)),
        check_vma=False,
    )
```

profile of v0, /device:TPU:0, one launch (start us, length us, event | category | flops | bytes accessed | tf_op | source)
XLA Modules:
  0.0 397.2 jit_solution(13419910968165939987)
XLA Ops:
  7.2 2.3 collective-permute-start.1
  9.5 0.7 fusion.21
  10.2 0.1 copy.14
  10.4 0.2 reduce-window.4
  10.6 0.1 fusion.18
  10.7 1.0 scatter_custom_fusion
  11.7 0.7 select_reduce_fusion
  12.4 15.4 %collective-permute-done.1 = bf16[128,6144]{1,0:T(8,128)(2,1)} collective-permute-done((bf16[128,6144]{1,0:T(8,128)(2,1)}, bf16[128,6144]{1,0:T(8,128)(2,1)}, u32[]{:S(2)}, u32[]{:S(2)}) %collective-permute-start.1) | collective-permute-done | bytes 1572896 | tf_op jit(solution)/shard_map/ppermute | solution.py:12
  27.8 1.8 multiply_convert_fusion
  29.5 1.6 gather_fusion.2
  31.2 0.8 gather_fusion
  32.0 0.2 copy-done
  32.2 1.1 broadcast_select_fusion
  33.3 0.0 all-gather.5.cloned.1.call-start
  33.3 0.7 all-gather.5.cloned.1.call-update
  34.1 70.5 %all-gather.3.cloned.1.call-done = bf16[640,6144]{1,0:T(8,128)(2,1)} async-done(((bf16[40,6144]{1,0:T(8,128)(2,1)}), bf16[640,6144]{1,0:T(8,128)(2,1)}) %all-gather.3.cloned.1.call-update) | async-done | bytes 7864336 | tf_op jit(solution)/shard_map/all_gather | solution.py:55
  104.6 8.5 %fusion.8 = f32[640,512]{1,0:T(8,128)S(1)} fusion(bf16[640,6144]{1,0:T(8,128)(2,1)} %all-gather.3.cloned.1.call-done, bf16[1,6144,512]{2,1,0:T(8,128)(2,1)} %param.11), kind=kOutput, calls=%fused_computation.15 | convolution fusion | flops 4026531840 | bytes 15466496 | tf_op jit(solution)/shard_map/dot_general | solution.py:58
  113.1 6.4 %fusion.4 = f32[640,512]{1,0:T(8,128)S(1)} fusion(bf16[640,6144]{1,0:T(8,128)(2,1)S(1)} %copy-done.2, bf16[1,6144,512]{2,1,0:T(8,128)(2,1)} %param.12), kind=kOutput, calls=%fused_computation.11 | convolution fusion | flops 4026531840 | bytes 15466496 | tf_op jit(solution)/shard_map/dot_general | solution.py:59
  119.6 56.0 %all-gather.5.cloned.1.call-done = bf16[640,6144]{1,0:T(8,128)(2,1)} async-done(((bf16[40,6144]{1,0:T(8,128)(2,1)}), bf16[640,6144]{1,0:T(8,128)(2,1)}) %all-gather.5.cloned.1.call-update) | async-done | bytes 7864336 | tf_op jit(solution)/shard_map/all_gather | solution.py:75
  175.6 8.5 %fusion = f32[640,512]{1,0:T(8,128)S(1)} fusion(bf16[640,6144]{1,0:T(8,128)(2,1)} %all-gather.5.cloned.1.call-done, bf16[1,512,6144]{2,1,0:T(8,128)(2,1)} %param.13), kind=kOutput, calls=%fused_computation.7 | convolution fusion | flops 4026531840 | bytes 15466496 | tf_op jit(solution)/shard_map/dot_general | solution.py:78
  184.0 1.0 copy-done.1
  185.1 10.6 %fusion.6 = f32[640,6144]{1,0:T(8,128)} fusion(bf16[1,6144,512]{2,1,0:T(8,128)(2,1)} %param.11, f32[640,512]{1,0:T(8,128)S(1)} %fusion.8, f32[640,512]{1,0:T(8,128)S(1)} %fusion, f32[640,512]{1,0:T(8,128)S(1)} %fusion.4), kind=kOutput, calls=%fused_computation.13 | convolution fusion | flops 4029808640 | bytes 25952256 | tf_op jit(solution)/shard_map/dot_general | solution.py:88
  195.7 15.1 %add_convert_fusion = bf16[640,6144]{1,0:T(8,128)(2,1)} fusion(f32[640,6144]{1,0:T(8,128)} %fusion.6, bf16[1,6144,512]{2,1,0:T(8,128)(2,1)} %param.12, f32[640,512]{1,0:T(8,128)} %copy-done.1, f32[640,512]{1,0:T(8,128)S(1)} %fusion.8), kind=kOutput, calls=%fused_computation.5 | convolution fusion | flops 4036362240 | bytes 32505856 | tf_op jit(solution)/shard_map/dot_general | solution.py:89
  210.8 0.2 reduce-scatter.7.cloned.1.call-start
  211.0 9.2 %convolution_convert_fusion = bf16[640,6144]{1,0:T(8,128)(2,1)} fusion(bf16[1,512,6144]{2,1,0:T(8,128)(2,1)} %param.13, f32[640,512]{1,0:T(8,128)S(1)} %fusion.4, f32[640,512]{1,0:T(8,128)S(1)} %fusion.8), kind=kOutput, calls=%fused_computation.6 | convolution fusion | flops 4032430080 | bytes 16777216 | tf_op jit(solution)/shard_map/dot_general | solution.py:66
  220.2 75.2 %reduce-scatter.9.cloned.1.call-done = bf16[40,6144]{1,0:T(8,128)(2,1)} async-done(((bf16[640,6144]{1,0:T(8,128)(2,1)}), bf16[40,6144]{1,0:T(8,128)(2,1)}) %reduce-scatter.9.cloned.1.call-update) | async-done | bytes 491536
  295.4 4.1 %gather_fusion.3 = bf16[128,6144]{1,0:T(8,128)(2,1)S(1)} fusion(bf16[40,6144]{1,0:T(8,128)(2,1)} %reduce-scatter.9.cloned.1.call-done, s32[1024]{0:T(1024)S(1)} %pad_clamp_fusion), kind=kCustom, calls=%fused_computation.3 | custom fusion | bytes 3146240 | tf_op jit(solution)/shard_map/gather | solution.py:94
  299.5 1.5 fusion.10
  301.0 81.9 %reduce-scatter.7.cloned.1.call-done = bf16[40,6144]{1,0:T(8,128)(2,1)} async-done(((bf16[640,6144]{1,0:T(8,128)(2,1)}), bf16[40,6144]{1,0:T(8,128)(2,1)}) %reduce-scatter.7.cloned.1.call-update) | async-done | bytes 491536
  383.0 1.1 convert_element_type.68
  384.1 3.2 gather_fusion.1
  387.2 3.4 fusion.12
  (17 shorter events, 0.2 us)
Async XLA Ops:
  7.2 97.4 %all-gather.3.cloned.1.call-start = ((), (), s32[]{:S(2)}) async-start(), calls=%async_computation.2 | async-start | bytes 8355840 | tf_op jit(solution)/shard_map/all_gather | solution.py:55
  7.2 20.6 %collective-permute-start.1 = (bf16[128,6144]{1,0:T(8,128)(2,1)}, bf16[128,6144]{1,0:T(8,128)(2,1)}, u32[]{:S(2)}, u32[]{:S(2)}) collective-permute-start(bf16[128,6144]{1,0:T(8,128)(2,1)} %bitcast.33), channel_id=1, source_target_pairs={{0,112},{16,0},{32,16},{48,32},{64,48},{80,64},{96,80},{112,96},{1... | collective-permute-start | bytes 4718600 | tf_op jit(solution)/shard_map/ppermute | solution.py:12
  9.5 21.6 %collective-permute-start = (bf16[128,6144]{1,0:T(8,128)(2,1)}, bf16[128,6144]{1,0:T(8,128)(2,1)S(1)}, u32[]{:S(2)}, u32[]{:S(2)}) collective-permute-start(bf16[128,6144]{1,0:T(8,128)(2,1)} %bitcast.34), channel_id=1, source_target_pairs={{0,16},{16,32},{32,48},{48,64},{64,80},{80,96},{96,112},{112,0},{1... | collective-permute-start | bytes 4718600 | tf_op jit(solution)/shard_map/ppermute | solution.py:12
  31.2 1.0 copy-start
  33.3 142.3 %all-gather.5.cloned.1.call-start = ((), (), s32[]{:S(2)}) async-start(), calls=%async_computation.3 | async-start | bytes 8355840 | tf_op jit(solution)/shard_map/all_gather | solution.py:75
  34.1 261.4 %reduce-scatter.9.cloned.1.call-start = ((), (), s32[]{:S(2)}) async-start(), calls=%async_computation.5 | async-start | bytes 8355840
  104.6 8.5 %copy-start.2 = (bf16[640,6144]{1,0:T(8,128)(2,1)S(1)}, bf16[640,6144]{1,0:T(8,128)(2,1)}, u32[]{:S(2)}) copy-start(bf16[640,6144]{1,0:T(8,128)(2,1)} %all-gather.3.cloned.1.call-done) | copy-start | bytes 23592964
  184.0 1.1 copy-start.1
  210.8 172.2 %reduce-scatter.7.cloned.1.call-start = ((), (), s32[]{:S(2)}) async-start(), calls=%async_computation.4 | async-start | bytes 8355840
Sparse Core Ops, SparseCore 0:
  33.4 71.1 all-gather.2
  107.3 68.1 all-gather.4
  210.9 84.4 reduce-scatter.8
  298.8 84.1 reduce-scatter.6
where the time goes:
time: 398 us; the launch traced here: 397 us
  waiting for transfers between devices  300 us (75%)
  matrix products  58.3 us (15%)
  between operations  13.9 us (3%)
  local copies, waits for them, and re-layouts  12.1 us (3%)
  other arithmetic  10.6 us (3%)
    unnamed x6, waiting for transfers between devices  158 us
    all_gather x1, waiting for transfers between devices, body(): all_acts = lax.all_gather(slot_acts, 'expert', axis=0, tiled=True)  70.5 us
    all_gather x1, waiting for transfers between devices, body(): all_grads = lax.all_gather(slot_grads, 'expert', axis=0, tiled=True)  56 us
    ppermute x2, waiting for transfers between devices, shifted(): return lax.ppermute(value, axis, pairs)  15.4 us
    dot_general x1, matrix products, backward_term(): lax.dot_general(up_grad, up_cols, contract, preferred_element_type=jnp.fl...  15.1 us
    dot_general x1, matrix products, backward_term(): lax.dot_general(gate_grad, gate_cols, contract, preferred_element_type=jn...  10.6 us
    dot_general x1, matrix products, forward_term(): return jnp.dot(hidden, down_rows, preferred_element_type=jnp.float32)  9.21 us
    dot_general x1, matrix products, forward_rows(): pre_gate = jnp.dot(rows_in, gate_cols, preferred_element_type=jnp.float32)  8.51 us
  transfers between devices with their start and end apart: 6, of which 5 were waited for; matrix products, arithmetic and copies ran while one was open for 9% of the time, Pallas kernels for 0%

commit v1 on v0

--- a/solution.py
+++ b/solution.py
@@ -52,7 +52,11 @@
     filled_slot = table >= 0
     source = jnp.maximum(table, 0)
     slot_acts = jnp.where(filled_slot[:, None], incoming[source], jnp.zeros((), incoming.dtype))
-    all_acts = lax.all_gather(slot_acts, "expert", axis=0, tiled=True)
+    count_2 = lax.axis_size("expert")
+    repeats = [count_2 if d == 0 else 1 for d in range(slot_acts.ndim)]
+    all_acts = lax.all_to_all(
+        jnp.tile(slot_acts, repeats), "expert", split_axis=0, concat_axis=0, tiled=True
+    )
 
     def forward_rows(rows_in):
         pre_gate = jnp.dot(rows_in, gate_cols, preferred_element_type=jnp.float32)

time: 398 us -> 358 us (0.90)
  waiting for transfers between devices: 300 us -> 156 us
  blocking collectives: 0 us -> 111 us
  matrix products: 58.3 us -> 50.3 us
    all_to_all x0 -> x1, blocking collectives: none -> 111 us  [body(): lax.all_to_all(jnp.tile(slot_acts, repeats), 'expert', split_axis=0, conc...]
    all_gather x1 -> x0, waiting for transfers between devices: 70.5 us -> none  [body(): all_acts = lax.all_gather(slot_acts, 'expert', axis=0, tiled=True)]
    all_gather x1, waiting for transfers between devices: 56 us -> 9.35 us  [body(): all_grads = lax.all_gather(slot_grads, 'expert', axis=0, tiled=True)]
    unnamed x6 -> x5, waiting for transfers between devices: 158 us -> 131 us
    dot_general x1, matrix products: 8.51 us -> 4.26 us  [forward_rows(): pre_gate = jnp.dot(rows_in, gate_cols, preferred_element_type=jnp.float32)]
  transfers between devices with their start and end apart: 6 -> 5, of which waited for: 5 -> 4; matrix products, arithmetic and copies ran while one was open for 9% -> 18% of each run, Pallas kernels for 0% -> 0%
where the time goes in v1:
time: 358 us
  waiting for transfers between devices  156 us (44%)
  blocking collectives  111 us (31%)
  matrix products  50.3 us (14%)
  between operations  13.9 us (4%)
  local copies, waits for them, and re-layouts  13.1 us (4%)
  other arithmetic  10.4 us (3%)
    unnamed x5, waiting for transfers between devices  131 us
    all_to_all x1, blocking collectives, body(): lax.all_to_all(jnp.tile(slot_acts, repeats), 'expert', split_axis=0, conc...  111 us
    dot_general x1, matrix products, backward_term(): lax.dot_general(up_grad, up_cols, contract, preferred_element_type=jnp.fl...  15.8 us
    ppermute x2, waiting for transfers between devices, shifted(): return lax.ppermute(value, axis, pairs)  15.4 us
    dot_general x1, matrix products, backward_term(): lax.dot_general(gate_grad, gate_cols, contract, preferred_element_type=jn...  11 us
    all_gather x1, waiting for transfers between devices, body(): all_grads = lax.all_gather(slot_grads, 'expert', axis=0, tiled=True)  9.35 us
    dot_general x1, matrix products, backward_rows(): lax.dot_general(grads_in, down_rows, contract, preferred_element_type=jnp...  8.45 us
  transfers between devices with their start and end apart: 5, of which 4 were waited for; matrix products, arithmetic and copies ran while one was open for 18% of the time, Pallas kernels for 0%

profile of v1, /device:TPU:0, one launch (start us, length us, event | category | flops | bytes accessed | tf_op | source)
XLA Modules:
  0.0 357.6 jit_solution(16803776809343478851)
XLA Ops:
  7.2 2.3 collective-permute-start.1
  9.5 0.7 fusion.21
  10.2 0.1 copy.14
  10.4 0.2 reduce-window.4
  10.6 0.1 fusion.18
  10.7 1.0 scatter_custom_fusion
  11.7 0.7 select_reduce_fusion
  12.4 15.4 %collective-permute-done.1 = bf16[128,6144]{1,0:T(8,128)(2,1)} collective-permute-done((bf16[128,6144]{1,0:T(8,128)(2,1)}, bf16[128,6144]{1,0:T(8,128)(2,1)}, u32[]{:S(2)}, u32[]{:S(2)}) %collective-permute-start.1) | collective-permute-done | bytes 1572896 | tf_op jit(solution)/shard_map/ppermute | solution.py:12
  27.8 1.8 multiply_convert_fusion
  29.5 1.6 gather_fusion.2
  31.2 0.8 gather_fusion
  32.0 0.2 copy-done
  32.2 0.9 broadcast_select_fusion
  33.1 0.0 reduce-scatter.7.cloned.1.call-start
  33.2 1.0 tile.2
  34.2 111.5 %all_to_all.9 = bf16[16,40,6144]{2,1,0:T(8,128)(2,1)S(1)} all-to-all(bf16[16,40,6144]{2,1,0:T(8,128)(2,1)S(1)} %tile.2), channel_id=1, replica_groups=mesh['section'=8,'expert'=16] {'expert'}, dimensions={0} | all-to-all | bytes 15728640 | tf_op jit(solution)/shard_map/all_to_all | solution.py:57
  145.7 4.3 %fusion.8 = f32[640,512]{1,0:T(8,128)S(1)} fusion(bf16[640,6144]{1,0:T(8,128)(2,1)S(1)} %bitcast.33, bf16[1,6144,512]{2,1,0:T(8,128)(2,1)S(1)} %bitcast.36), kind=kOutput, calls=%fused_computation.15 | convolution fusion | flops 4026531840 | bytes 15466496 | tf_op jit(solution)/shard_map/dot_general | solution.py:62
  150.0 4.2 %fusion.4 = f32[640,512]{1,0:T(8,128)S(1)} fusion(bf16[640,6144]{1,0:T(8,128)(2,1)S(1)} %bitcast.34, bf16[1,6144,512]{2,1,0:T(8,128)(2,1)S(1)} %bitcast.41), kind=kOutput, calls=%fused_computation.11 | convolution fusion | flops 4026531840 | bytes 15466496 | tf_op jit(solution)/shard_map/dot_general | solution.py:63
  154.2 6.5 %convolution_convert_fusion = bf16[640,6144]{1,0:T(8,128)(2,1)} fusion(bf16[1,512,6144]{2,1,0:T(8,128)(2,1)S(1)} %bitcast.39, f32[640,512]{1,0:T(8,128)S(1)} %fusion.4, f32[640,512]{1,0:T(8,128)S(1)} %fusion.8), kind=kOutput, calls=%fused_computation.6 | convolution fusion | flops 4032430080 | bytes 16777216 | tf_op jit(solution)/shard_map/dot_general | solution.py:70
  160.8 0.2 reduce-scatter.9.cloned.1.call-start
  161.0 9.3 %all-gather.2.cloned.1.call-done = bf16[640,6144]{1,0:T(8,128)(2,1)} async-done(((bf16[40,6144]{1,0:T(8,128)(2,1)}), bf16[640,6144]{1,0:T(8,128)(2,1)}) %all-gather.2.cloned.1.call-update) | async-done | bytes 7864336 | tf_op jit(solution)/shard_map/all_gather | solution.py:79
  170.3 8.5 %fusion = f32[640,512]{1,0:T(8,128)S(1)} fusion(bf16[640,6144]{1,0:T(8,128)(2,1)} %all-gather.2.cloned.1.call-done, bf16[1,512,6144]{2,1,0:T(8,128)(2,1)} %param.13), kind=kOutput, calls=%fused_computation.7 | convolution fusion | flops 4026531840 | bytes 15466496 | tf_op jit(solution)/shard_map/dot_general | solution.py:82
  178.8 1.0 copy-done.1
  179.9 11.0 %fusion.6 = f32[640,6144]{1,0:T(8,128)} fusion(bf16[1,6144,512]{2,1,0:T(8,128)(2,1)} %param.11, f32[640,512]{1,0:T(8,128)S(1)} %fusion.8, f32[640,512]{1,0:T(8,128)S(1)} %fusion, f32[640,512]{1,0:T(8,128)S(1)} %fusion.4), kind=kOutput, calls=%fused_computation.13 | convolution fusion | flops 4029808640 | bytes 25952256 | tf_op jit(solution)/shard_map/dot_general | solution.py:92
  190.9 15.8 %add_convert_fusion = bf16[640,6144]{1,0:T(8,128)(2,1)} fusion(f32[640,6144]{1,0:T(8,128)} %fusion.6, bf16[1,6144,512]{2,1,0:T(8,128)(2,1)} %param.12, f32[640,512]{1,0:T(8,128)} %copy-done.1, f32[640,512]{1,0:T(8,128)S(1)} %fusion.8), kind=kOutput, calls=%fused_computation.5 | convolution fusion | flops 4036362240 | bytes 32505856 | tf_op jit(solution)/shard_map/dot_general | solution.py:93
  206.8 51.0 %reduce-scatter.7.cloned.1.call-done = bf16[40,6144]{1,0:T(8,128)(2,1)} async-done(((bf16[640,6144]{1,0:T(8,128)(2,1)}), bf16[40,6144]{1,0:T(8,128)(2,1)}) %reduce-scatter.7.cloned.1.call-update) | async-done | bytes 491536
  257.7 1.1 convert_element_type.68
  258.8 3.2 gather_fusion.1
  262.0 3.4 fusion.12
  265.4 80.1 %reduce-scatter.9.cloned.1.call-done = bf16[40,6144]{1,0:T(8,128)(2,1)} async-done(((bf16[640,6144]{1,0:T(8,128)(2,1)}), bf16[40,6144]{1,0:T(8,128)(2,1)}) %reduce-scatter.9.cloned.1.call-update) | async-done | bytes 491536
  345.5 4.1 %gather_fusion.3 = bf16[128,6144]{1,0:T(8,128)(2,1)S(1)} fusion(bf16[40,6144]{1,0:T(8,128)(2,1)} %reduce-scatter.9.cloned.1.call-done, s32[1024]{0:T(1024)S(1)} %pad_clamp_fusion), kind=kCustom, calls=%fused_computation.3 | custom fusion | bytes 3146240 | tf_op jit(solution)/shard_map/gather | solution.py:98
  349.6 1.5 fusion.10
  (29 shorter events, 0.2 us)
Async XLA Ops:
  7.2 163.2 %all-gather.2.cloned.1.call-start = ((), (), s32[]{:S(2)}) async-start(), calls=%async_computation.3 | async-start | bytes 8355840 | tf_op jit(solution)/shard_map/all_gather | solution.py:79
  7.2 20.6 %collective-permute-start.1 = (bf16[128,6144]{1,0:T(8,128)(2,1)}, bf16[128,6144]{1,0:T(8,128)(2,1)}, u32[]{:S(2)}, u32[]{:S(2)}) collective-permute-start(bf16[128,6144]{1,0:T(8,128)(2,1)} %bitcast.42), channel_id=1, source_target_pairs={{0,112},{16,0},{32,16},{48,32},{64,48},{80,64},{96,80},{112,96},{1... | collective-permute-start | bytes 4718600 | tf_op jit(solution)/shard_map/ppermute | solution.py:12
  9.5 21.6 %collective-permute-start = (bf16[128,6144]{1,0:T(8,128)(2,1)}, bf16[128,6144]{1,0:T(8,128)(2,1)S(1)}, u32[]{:S(2)}, u32[]{:S(2)}) collective-permute-start(bf16[128,6144]{1,0:T(8,128)(2,1)} %bitcast.43), channel_id=1, source_target_pairs={{0,16},{16,32},{32,48},{48,64},{64,80},{80,96},{96,112},{112,0},{1... | collective-permute-start | bytes 4718600 | tf_op jit(solution)/shard_map/ppermute | solution.py:12
  31.2 1.0 copy-start
  33.1 224.6 %reduce-scatter.7.cloned.1.call-start = ((), (), s32[]{:S(2)}) async-start(), calls=%async_computation.4 | async-start | bytes 8355840
  33.2 112.5 %slice-start = ((s8[6291456]{0:T(1024)(128)(4,1)}), s8[4194304]{0:T(1024)(128)(4,1)S(1)}, s32[]{:S(2)}) async-start(s8[6291456]{0:T(1024)(128)(4,1)} %bitcast.35), calls=%async_computation.6 | async-start | bytes 8388608
  34.2 111.5 %slice-start.1 = ((s8[6291456]{0:T(1024)(128)(4,1)}), s8[2097152]{0:T(1024)(128)(4,1)S(1)}, s32[]{:S(2)}) async-start(s8[6291456]{0:T(1024)(128)(4,1)} %bitcast.35), calls=%async_computation.7 | async-start | bytes 4194304
  34.2 115.8 %slice-start.4 = ((s8[6291456]{0:T(1024)(128)(4,1)}), s8[4194304]{0:T(1024)(128)(4,1)S(1)}, s32[]{:S(2)}) async-start(s8[6291456]{0:T(1024)(128)(4,1)} %bitcast.40), calls=%async_computation.10 | async-start | bytes 8388608
  145.7 4.3 %slice-start.5 = ((s8[6291456]{0:T(1024)(128)(4,1)}), s8[2097152]{0:T(1024)(128)(4,1)S(1)}, s32[]{:S(2)}) async-start(s8[6291456]{0:T(1024)(128)(4,1)} %bitcast.40), calls=%async_computation.11 | async-start | bytes 4194304
  145.7 8.5 %slice-start.2 = ((s8[6291456]{0:T(1024)(128)(4,1)}), s8[4194304]{0:T(1024)(128)(4,1)S(1)}, s32[]{:S(2)}) async-start(s8[6291456]{0:T(1024)(128)(4,1)} %bitcast.38), calls=%async_computation.8 | async-start | bytes 8388608
  150.0 4.2 %slice-start.3 = ((s8[6291456]{0:T(1024)(128)(4,1)}), s8[2097152]{0:T(1024)(128)(4,1)S(1)}, s32[]{:S(2)}) async-start(s8[6291456]{0:T(1024)(128)(4,1)} %bitcast.38), calls=%async_computation.9 | async-start | bytes 4194304
  160.8 184.7 %reduce-scatter.9.cloned.1.call-start = ((), (), s32[]{:S(2)}) async-start(), calls=%async_computation.5 | async-start | bytes 8355840
  178.8 1.1 copy-start.1
Sparse Core Ops, SparseCore 0:
  33.3 137.0 all-gather.1
  173.9 83.8 reduce-scatter.6
  261.2 84.1 reduce-scatter.8
